TPU v7x, 32 devices: a whole 2x2x4 slice. The times are simulated.
32 devices in a mesh: fsdp: 32 (over z, y, x, core).
Axes of the slice: x: 2, y: 2, z: 4, core: 2. Of those that a mesh axis runs over, the one named last changes fastest.
Arguments:
- block_input: bfloat16 [32, 784, 768], P('fsdp'), may hold values from -6 to 6
- seg_ids: int32 [32, 784], P('fsdp'), may hold values from 0 to 3, as said below
- gain_attn: bfloat16 [768], P('fsdp'), may hold values from 0.099609375 to 1.8984375
- w_query: bfloat16 [768, 768], P('fsdp'), may hold values from -0.21875 to 0.21875
- w_key: bfloat16 [768, 768], P('fsdp'), may hold values from -0.21875 to 0.21875
- w_value: bfloat16 [768, 768], P('fsdp'), may hold values from -0.21875 to 0.21875
- w_out: bfloat16 [768, 768], P('fsdp'), may hold values from -0.875 to 0.875
- gain_ffn: bfloat16 [768], P('fsdp'), may hold values from 0.099609375 to 1.8984375
- w_gate: bfloat16 [768, 2048], P('fsdp'), may hold values from -0.21875 to 0.21875
- w_up: bfloat16 [768, 2048], P('fsdp'), may hold values from -0.21875 to 0.21875
- w_down: bfloat16 [2048, 768], P('fsdp'), may hold values from -0.125 to 0.125
- cotangent: bfloat16 [32, 784, 768], P('fsdp'), may hold values from -6 to 6
Outputs:
- block_output: bfloat16 [32, 784, 768], P('fsdp')
- input_grad: bfloat16 [32, 784, 768], P('fsdp')
- gain_attn_grad: float32 [768], P('fsdp')
- w_query_grad: float32 [768, 768], P('fsdp')
- w_key_grad: float32 [768, 768], P('fsdp')
- w_value_grad: float32 [768, 768], P('fsdp')
- w_out_grad: float32 [768, 768], P('fsdp')
- gain_ffn_grad: float32 [768], P('fsdp')
- w_gate_grad: float32 [768, 2048], P('fsdp')
- w_up_grad: float32 [768, 2048], P('fsdp')
- w_down_grad: float32 [2048, 768], P('fsdp')
Inputs may be any that keep to these rules, and one draw needn't show every extreme that they name: `seg_ids`: each row holds, from slot 0 on, either one image of 577 tokens (segment 0) or two or three images of 257 tokens (segments 0, 1, 2 in order), and padding with segment number 3 in all remaining slots, at least one of them.
All inputs are finite; a program needn't handle non-finite values.
Results may differ from a plain program's by a relative error of at most 0.015.
Values may be sent and summed in bfloat16 or wider, within the bound.
A program may use at most 128 MiB of HBM per device.

v0:
```python
from functools import partial

import jax
import jax.numpy as jnp
from jax import lax
from jax.sharding import PartitionSpec as P

HEAD = 64


EPSILON = 1e-05


def rope_tables(segment_row, head_size):
    length = segment_row.shape[0]
    places = jnp.arange(length, dtype=jnp.int32)
    labels = jnp.arange(4, dtype=jnp.int32)
    counts = jnp.sum((segment_row[:, None] == labels[None, :]).astype(jnp.int32), axis=0)
    before = (labels[None, :] < segment_row[:, None]).astype(jnp.int32)
    starts = jnp.sum(before * counts[None, :], axis=1)
    offsets = (places - starts).astype(jnp.float32)
    frequency = 10000.0 ** (-(jnp.arange(head_size // 2, dtype=jnp.float32) * 2.0) / head_size)
    angles = offsets[:, None] * frequency[None, :]
    return (jnp.cos(angles), jnp.sin(angles))


def rotate(values, cosine, sine_table):
    half_size = values.shape[-1] // 2
    lower_half = values[..., :half_size]
    upper_half = values[..., half_size:]
    cosine = cosine[..., None, :]
    sine_table = sine_table[..., None, :]
    return jnp.concatenate(
        [
            lower_half * cosine - upper_half * sine_table,
            upper_half * cosine + lower_half * sine_table,
        ],
        axis=-1,
    )


def unrotate(gradient, cosine, sine_table):
    half_size = gradient.shape[-1] // 2
    lower_half = gradient[..., :half_size]
    upper_half = gradient[..., half_size:]
    cosine = cosine[..., None, :]
    sine_table = sine_table[..., None, :]
    return jnp.concatenate(
        [
            lower_half * cosine + upper_half * sine_table,
            upper_half * cosine - lower_half * sine_table,
        ],
        axis=-1,
    )


def head_forward(query_head, key_head, value_head, allowed, score_scale):
    raw_scores = jnp.einsum("le,me->lm", query_head, key_head, preferred_element_type=jnp.float32)
    masked = jnp.where(allowed, raw_scores * score_scale, -1e30)
    highest = jnp.max(masked, axis=-1, keepdims=True)
    exponent = jnp.exp(masked - highest)
    denominator = jnp.sum(exponent, axis=-1, keepdims=True)
    weights = (exponent / denominator).astype(jnp.bfloat16)
    mixture = jnp.dot(weights, value_head, preferred_element_type=jnp.float32)
    return (mixture, (highest + jnp.log(denominator))[:, 0])


def head_backward(query_head, key_head, value_head, grad_head, logsum, allowed, score_scale):
    raw_scores = jnp.einsum("le,me->lm", query_head, key_head, preferred_element_type=jnp.float32)
    masked = jnp.where(allowed, raw_scores * score_scale, -1e30)
    probabilities = jnp.exp(masked - logsum[:, None])
    weights = probabilities.astype(jnp.bfloat16)
    grad_value = jnp.einsum("lm,le->me", weights, grad_head, preferred_element_type=jnp.float32)
    grad_probs = jnp.einsum("le,me->lm", grad_head, value_head, preferred_element_type=jnp.float32)
    grad_scores = probabilities * (
        grad_probs - jnp.sum(grad_probs * probabilities, axis=-1, keepdims=True)
    )
    grad_scores = grad_scores.astype(jnp.bfloat16)
    grad_query = jnp.dot(grad_scores, key_head, preferred_element_type=jnp.float32) * score_scale
    grad_key = (
        jnp.einsum("lm,le->me", grad_scores, query_head, preferred_element_type=jnp.float32)
        * score_scale
    )
    return (grad_query, grad_key, grad_value)


def norm_backward(grad_normed, normed, inverse, gain):
    scaled = grad_normed * gain
    return inverse * (scaled - normed * jnp.mean(scaled * normed, axis=-1, keepdims=True))


def per_device(
    block_input,
    seg_ids,
    gain_attn,
    w_query,
    w_key,
    w_value,
    w_out,
    gain_ffn,
    w_gate,
    w_up,
    w_down,
    cotangent,
):
    row_count, length, width = block_input.shape
    head_count = width // HEAD
    tokens = row_count * length
    score_scale = HEAD ** (-0.5)
    attn_set = (
        lax.all_gather(gain_attn, "fsdp", axis=0, tiled=True),
        lax.all_gather(w_query, "fsdp", axis=0, tiled=True),
        lax.all_gather(w_key, "fsdp", axis=0, tiled=True),
        lax.all_gather(w_value, "fsdp", axis=0, tiled=True),
        lax.all_gather(w_out, "fsdp", axis=0, tiled=True),
    )
    ffn_set = (
        lax.all_gather(gain_ffn, "fsdp", axis=0, tiled=True),
        lax.all_gather(w_gate, "fsdp", axis=0, tiled=True),
        lax.all_gather(w_up, "fsdp", axis=0, tiled=True),
        lax.all_gather(w_down, "fsdp", axis=0, tiled=True),
    )
    cosine, sine_table = jax.vmap(partial(rope_tables, head_size=HEAD))(seg_ids)
    places = jnp.arange(length, dtype=jnp.int32)
    allowed = (seg_ids[:, :, None] == seg_ids[:, None, :]) & (
        places[None, None, :] <= places[None, :, None]
    )
    inputs = block_input.reshape(tokens, width).astype(jnp.float32)
    scale_one = lax.rsqrt(jnp.mean(inputs * inputs, axis=-1, keepdims=True) + EPSILON)
    normed_one = inputs * scale_one
    normed_low = (normed_one * attn_set[0].astype(jnp.float32)).astype(jnp.bfloat16)
    queries = jnp.dot(normed_low, attn_set[1], preferred_element_type=jnp.float32).reshape(
        row_count, length, head_count, HEAD
    )
    key_vectors = jnp.dot(normed_low, attn_set[2], preferred_element_type=jnp.float32).reshape(
        row_count, length, head_count, HEAD
    )
    value_vectors = jnp.dot(normed_low, attn_set[3], preferred_element_type=jnp.float32).astype(
        jnp.bfloat16
    )
    value_vectors = value_vectors.reshape(row_count, length, head_count, HEAD)
    query_rot = rotate(queries, cosine, sine_table).astype(jnp.bfloat16)
    key_rot = rotate(key_vectors, cosine, sine_table).astype(jnp.bfloat16)
    query_heads = jnp.moveaxis(query_rot, 2, 1)
    key_heads = jnp.moveaxis(key_rot, 2, 1)
    value_heads = jnp.moveaxis(value_vectors, 2, 1)

    def row_forward(operands):
        query_row, key_row, value_row, allowed_row = operands

        def one_head(head_parts):
            return head_forward(
                head_parts[0], head_parts[1], head_parts[2], allowed_row, score_scale
            )

        return lax.map(one_head, (query_row, key_row, value_row))

    mixture, logsum = lax.map(row_forward, (query_heads, key_heads, value_heads, allowed))
    attn_low = jnp.moveaxis(mixture, 1, 2).reshape(tokens, width).astype(jnp.bfloat16)
    middle = inputs + jnp.dot(attn_low, attn_set[4], preferred_element_type=jnp.float32)
    scale_two = lax.rsqrt(jnp.mean(middle * middle, axis=-1, keepdims=True) + EPSILON)
    normed_two = middle * scale_two
    ffn_low = (normed_two * ffn_set[0].astype(jnp.float32)).astype(jnp.bfloat16)
    gate_proj = jnp.dot(ffn_low, ffn_set[1], preferred_element_type=jnp.float32)
    up_proj = jnp.dot(ffn_low, ffn_set[2], preferred_element_type=jnp.float32)
    gate_sigm = jax.nn.sigmoid(gate_proj)
    activated = gate_proj * gate_sigm
    hidden = (activated * up_proj).astype(jnp.bfloat16)
    output_full = middle + jnp.dot(hidden, ffn_set[3], preferred_element_type=jnp.float32)
    output = output_full.astype(jnp.bfloat16).reshape(row_count, length, width)
    grad_out = cotangent.reshape(tokens, width).astype(jnp.float32)
    grad_low = grad_out.astype(jnp.bfloat16)
    down_grad = jnp.einsum("tf,td->fd", hidden, grad_low, preferred_element_type=jnp.float32)
    grad_hidden = jnp.einsum("td,fd->tf", grad_low, ffn_set[3], preferred_element_type=jnp.float32)
    gate_grad_low = (
        grad_hidden * up_proj * gate_sigm * (1.0 + gate_proj * (1.0 - gate_sigm))
    ).astype(jnp.bfloat16)
    up_grad_low = (grad_hidden * activated).astype(jnp.bfloat16)
    gate_grad = jnp.einsum("td,tf->df", ffn_low, gate_grad_low, preferred_element_type=jnp.float32)
    up_grad = jnp.einsum("td,tf->df", ffn_low, up_grad_low, preferred_element_type=jnp.float32)
    grad_normed_two = jnp.einsum(
        "tf,df->td", gate_grad_low, ffn_set[1], preferred_element_type=jnp.float32
    )
    grad_normed_two = grad_normed_two + jnp.einsum(
        "tf,df->td", up_grad_low, ffn_set[2], preferred_element_type=jnp.float32
    )
    gain_two_grad = jnp.sum(grad_normed_two * normed_two, axis=0)
    grad_middle = grad_out + norm_backward(
        grad_normed_two, normed_two, scale_two, ffn_set[0].astype(jnp.float32)
    )
    ffn_parts = (
        lax.psum_scatter(gain_two_grad, "fsdp", scatter_dimension=0, tiled=True),
        lax.psum_scatter(gate_grad, "fsdp", scatter_dimension=0, tiled=True),
        lax.psum_scatter(up_grad, "fsdp", scatter_dimension=0, tiled=True),
        lax.psum_scatter(down_grad, "fsdp", scatter_dimension=0, tiled=True),
    )
    branch_low = grad_middle.astype(jnp.bfloat16)
    out_grad = jnp.einsum("te,td->ed", attn_low, branch_low, preferred_element_type=jnp.float32)
    grad_attn = jnp.einsum(
        "td,ed->te", branch_low, attn_set[4], preferred_element_type=jnp.float32
    ).astype(jnp.bfloat16)
    grad_heads = jnp.moveaxis(grad_attn.reshape(row_count, length, head_count, HEAD), 2, 1)

    def row_backward(operands):
        query_row, key_row, value_row, grad_row, logsum_row, allowed_row = operands

        def one_head(head_parts):
            return head_backward(
                head_parts[0],
                head_parts[1],
                head_parts[2],
                head_parts[3],
                head_parts[4],
                allowed_row,
                score_scale,
            )

        return lax.map(one_head, (query_row, key_row, value_row, grad_row, logsum_row))

    grad_query_heads, grad_key_heads, grad_value_heads = lax.map(
        row_backward, (query_heads, key_heads, value_heads, grad_heads, logsum, allowed)
    )
    query_grad_low = (
        unrotate(jnp.moveaxis(grad_query_heads, 1, 2), cosine, sine_table)
        .reshape(tokens, width)
        .astype(jnp.bfloat16)
    )
    key_grad_low = (
        unrotate(jnp.moveaxis(grad_key_heads, 1, 2), cosine, sine_table)
        .reshape(tokens, width)
        .astype(jnp.bfloat16)
    )
    value_grad_low = (
        jnp.moveaxis(grad_value_heads, 1, 2).reshape(tokens, width).astype(jnp.bfloat16)
    )
    query_grad = jnp.einsum(
        "td,te->de", normed_low, query_grad_low, preferred_element_type=jnp.float32
    )
    key_grad = jnp.einsum("td,te->de", normed_low, key_grad_low, preferred_element_type=jnp.float32)
    value_grad = jnp.einsum(
        "td,te->de", normed_low, value_grad_low, preferred_element_type=jnp.float32
    )
    grad_normed_one = jnp.einsum(
        "te,de->td", query_grad_low, attn_set[1], preferred_element_type=jnp.float32
    )
    grad_normed_one = grad_normed_one + jnp.einsum(
        "te,de->td", key_grad_low, attn_set[2], preferred_element_type=jnp.float32
    )
    grad_normed_one = grad_normed_one + jnp.einsum(
        "te,de->td", value_grad_low, attn_set[3], preferred_element_type=jnp.float32
    )
    gain_one_grad = jnp.sum(grad_normed_one * normed_one, axis=0)
    input_full = grad_middle + norm_backward(
        grad_normed_one, normed_one, scale_one, attn_set[0].astype(jnp.float32)
    )
    input_grad = input_full.astype(jnp.bfloat16).reshape(row_count, length, width)
    attn_parts = (
        lax.psum_scatter(gain_one_grad, "fsdp", scatter_dimension=0, tiled=True),
        lax.psum_scatter(query_grad, "fsdp", scatter_dimension=0, tiled=True),
        lax.psum_scatter(key_grad, "fsdp", scatter_dimension=0, tiled=True),
        lax.psum_scatter(value_grad, "fsdp", scatter_dimension=0, tiled=True),
        lax.psum_scatter(out_grad, "fsdp", scatter_dimension=0, tiled=True),
    )
    every = attn_parts + ffn_parts
    return (
        output,
        input_grad,
        every[0],
        every[1],
        every[2],
        every[3],
        every[4],
        every[5],
        every[6],
        every[7],
        every[8],
    )


def solution(mesh):
    placed = (
        P("fsdp", None, None),
        P("fsdp", None),
        P("fsdp"),
        P("fsdp", None),
        P("fsdp", None),
        P("fsdp", None),
        P("fsdp", None),
        P("fsdp"),
        P("fsdp", None),
        P("fsdp", None),
        P("fsdp", None),
        P("fsdp", None, None),
    )
    return jax.shard_map(
        per_device,
        mesh=mesh,
        in_specs=placed,
        out_specs=(
            P("fsdp", None, None),
            P("fsdp", None, None),
            P("fsdp"),
            P("fsdp", None),
            P("fsdp", None),
            P("fsdp", None),
            P("fsdp", None),
            P("fsdp"),
            P("fsdp", None),
            P("fsdp", None),
            P("fsdp", None),
        ),
        check_vma=False,
    )
```

profile of v0, /device:TPU:0, one launch (start us, length us, event | category | flops | bytes accessed | tf_op | source)
XLA Modules:
  0.0 1244.4 jit_solution(14992071916210314030)
XLA Ops:
  13.9 42.1 %all-reduce.5 = (bf16[768]{0:T(1024)(128)(2,1)S(1)}, bf16[768]{0:T(1024)(128)(2,1)S(1)}) all-reduce(bf16[768]{0:T(1024)(128)(2,1)S(1)} %dynamic-update-slice, bf16[768]{0:T(1024)(128)(2,1)S(1)} %dynamic-update-slice.1), channel_id=1, replica_groups=mesh['fsdp'=32] {'fsdp'}, use_global_device_ids=true, to_apply=%add | all-reduce | flops 1536 | bytes 6144
  58.2 9.6 all-gather.10.cloned.1.call-done
  70.1 53.5 %all-gather.8.cloned.1.call-done = bf16[768,768]{1,0:T(8,128)(2,1)} async-done(((bf16[24,768]{1,0:T(8,128)(2,1)}), bf16[768,768]{1,0:T(8,128)(2,1)}) %all-gather.8.cloned.1.call-update) | async-done | bytes 1179664 | tf_op jit(solution)/shard_map/all_gather | solution.py:112
  131.6 3.9 copy.56
  138.1 41.4 %all-gather.12.cloned.1.call-done = bf16[768,768]{1,0:T(8,128)(2,1)} async-done(((bf16[24,768]{1,0:T(8,128)(2,1)}), bf16[768,768]{1,0:T(8,128)(2,1)}) %all-gather.12.cloned.1.call-update) | async-done | bytes 1179664 | tf_op jit(solution)/shard_map/all_gather | solution.py:114
  185.3 54.6 %while.50 = (s32[]{:T(128)}, bf16[12,784,64]{1,2,0:T(8,128)(2,1)}, f32[12,784]{1,0:T(8,128)S(1)}, bf16[12,784,64]{2,1,0:T(8,128)(2,1)}, bf16[12,784,64]{2,1,0:T(...) while((s32[]{:T(128)}, bf16[12,784,64]{1,2,0:T(8,128)(2,1)}, ...), condition=%wide.region_6.7_spmd.clone.clone, body=%wide.region_3.6_spmd.clone.sunk.clone | while | flops 164112368 | bytes 8255313 | solution.py:156
  239.9 3.4 multiply_reduce_fusion.3
  245.0 50.8 %all-gather.16.cloned.1.call-done = bf16[768,2048]{1,0:T(8,128)(2,1)} async-done(((bf16[24,2048]{1,0:T(8,128)(2,1)}), bf16[768,2048]{1,0:T(8,128)(2,1)}) %all-gather.16.cloned.1.call-update) | async-done | bytes 3145744 | tf_op jit(solution)/shard_map/all_gather | solution.py:119
  295.9 6.4 fusion.95
  302.3 54.1 %all-gather.18.cloned.1.call-done = bf16[768,2048]{1,0:T(8,128)(2,1)} async-done(((bf16[24,2048]{1,0:T(8,128)(2,1)}), bf16[768,2048]{1,0:T(8,128)(2,1)}) %all-gather.18.cloned.1.call-update) | async-done | bytes 3145744 | tf_op jit(solution)/shard_map/all_gather | solution.py:120
  356.4 6.5 fusion.96
  362.9 54.1 %all-gather.20.cloned.1.call-done = bf16[2048,768]{1,0:T(8,128)(2,1)} async-done(((bf16[64,768]{1,0:T(8,128)(2,1)}), bf16[2048,768]{1,0:T(8,128)(2,1)}) %all-gather.20.cloned.1.call-update) | async-done | bytes 3145744 | tf_op jit(solution)/shard_map/all_gather | solution.py:121
  417.0 9.8 multiply_convert_fusion.1
  431.8 3.1 multiply_reduce_fusion.1
  439.9 3.8 convolution_convert_fusion
  446.6 114.9 %while.51 = (s32[]{:T(128)}, f32[12,784,64]{1,2,0:T(8,128)}, f32[12,784,64]{1,2,0:T(8,128)}, bf16[12,784,64]{1,2,0:T(8,128)(2,1)S(1)}, bf16[12,784,64]{2,1,0:T(8...) while((s32[]{:T(128)}, f32[12,784,64]{1,2,0:T(8,128)}, ...), condition=%wide.region_11.12_spmd.clone.clone, body=%wide.region_9.11_spmd.clone.sunk.clone | while | flops 400855296 | bytes 20741992 | solution.py:218
  561.5 4.2 multiply_add_fusion.1
  567.3 3.1 fusion.81
  576.2 4.4 fusion.79
  580.7 7.3 fusion.100
  588.1 7.3 fusion.101
  596.7 8.0 fusion.71
  610.5 3.3 fusion.64
  613.8 38.6 %all-reduce.4 = (f32[768]{0:T(1024)S(1)}, f32[768]{0:T(1024)S(1)}) all-reduce(f32[768]{0:T(1024)S(1)} %get-tuple-element.269, f32[768]{0:T(1024)S(1)} %get-tuple-element.267), channel_id=2, replica_groups=mesh['fsdp'=32] {'fsdp'}, use_global_device_ids=true, to_apply=%region_14.15.clone | all-reduce | flops 1536 | bytes 12288
  653.6 4.3 fusion.69
  657.9 5.6 fusion.68
  663.4 5.1 reduce-scatter.10.cloned.1.call-done
  668.6 103.8 %reduce-scatter.8.cloned.1.call-done = f32[24,768]{1,0:T(8,128)} async-done(((f32[768,768]{1,0:T(8,128)}), f32[24,768]{1,0:T(8,128)}) %reduce-scatter.8.cloned.1.call-update) | async-done | bytes 73744 | tf_op jit(solution)/shard_map/reduce_scatter | solution.py:259
  772.3 104.8 %reduce-scatter.12.cloned.1.call-done = f32[24,768]{1,0:T(8,128)} async-done(((f32[768,768]{1,0:T(8,128)}), f32[24,768]{1,0:T(8,128)}) %reduce-scatter.12.cloned.1.call-update) | async-done | bytes 73744 | tf_op jit(solution)/shard_map/reduce_scatter | solution.py:261
  877.1 119.4 %reduce-scatter.16.cloned.1.call-done = f32[24,2048]{1,0:T(8,128)} async-done(((f32[768,2048]{1,0:T(8,128)}), f32[24,2048]{1,0:T(8,128)}) %reduce-scatter.16.cloned.1.call-update) | async-done | bytes 196624 | tf_op jit(solution)/shard_map/reduce_scatter | solution.py:193
  996.6 120.9 %reduce-scatter.18.cloned.1.call-done = f32[24,2048]{1,0:T(8,128)} async-done(((f32[768,2048]{1,0:T(8,128)}), f32[24,2048]{1,0:T(8,128)}) %reduce-scatter.18.cloned.1.call-update) | async-done | bytes 196624 | tf_op jit(solution)/shard_map/reduce_scatter | solution.py:194
  1117.5 119.9 %reduce-scatter.20.cloned.1.call-done = f32[64,768]{1,0:T(8,128)} async-done(((f32[2048,768]{1,0:T(8,128)}), f32[64,768]{1,0:T(8,128)}) %reduce-scatter.20.cloned.1.call-update) | async-done | bytes 196624 | tf_op jit(solution)/shard_map/reduce_scatter | solution.py:195
  (282 shorter events, 226.2 us)
Async XLA Ops:
  7.2 48.8 %copy-start.2 = (bf16[1,784,768]{2,1,0:T(8,128)(2,1)S(1)}, bf16[1,784,768]{2,1,0:T(8,128)(2,1)}, u32[]{:S(2)}) copy-start(bf16[1,784,768]{2,1,0:T(8,128)(2,1)} %param.16) | copy-start | bytes 3612676
  7.2 49.1 %copy-start.21 = (s32[1,784]{1,0:T(1,128)S(1)}, s32[1,784]{1,0:T(1,128)}, u32[]{:S(2)}) copy-start(s32[1,784]{1,0:T(1,128)} %param.17) | copy-start | bytes 9412
  7.2 60.5 %all-gather.10.cloned.1.call-start = ((), (), s32[]{:S(2)}) async-start(), calls=%async_computation.8 | async-start | bytes 1216512 | tf_op jit(solution)/shard_map/all_gather | solution.py:113
  7.9 115.7 %all-gather.8.cloned.1.call-start = ((), (), s32[]{:S(2)}) async-start(), calls=%async_computation.7 | async-start | bytes 1216512 | tf_op jit(solution)/shard_map/all_gather | solution.py:112
  8.7 170.8 %all-gather.12.cloned.1.call-start = ((), (), s32[]{:S(2)}) async-start(), calls=%async_computation.9 | async-start | bytes 1216512 | tf_op jit(solution)/shard_map/all_gather | solution.py:114
  9.4 230.5 %all-gather.14.cloned.1.call-start = ((), (), s32[]{:S(2)}) async-start(), calls=%async_computation.10 | async-start | bytes 1216512 | tf_op jit(solution)/shard_map/all_gather | solution.py:115
  10.0 285.9 %all-gather.16.cloned.1.call-start = ((), (), s32[]{:S(2)}) async-start(), calls=%async_computation.11 | async-start | bytes 3244032 | tf_op jit(solution)/shard_map/all_gather | solution.py:119
  10.6 345.8 %all-gather.18.cloned.1.call-start = ((), (), s32[]{:S(2)}) async-start(), calls=%async_computation.12 | async-start | bytes 3244032 | tf_op jit(solution)/shard_map/all_gather | solution.py:120
  11.2 405.9 %all-gather.20.cloned.1.call-start = ((), (), s32[]{:S(2)}) async-start(), calls=%async_computation.13 | async-start | bytes 3244032 | tf_op jit(solution)/shard_map/all_gather | solution.py:121
  11.9 651.5 %reduce-scatter.14.cloned.1.call-start = ((), (), s32[]{:S(2)}) async-start(), calls=%async_computation.17 | async-start | bytes 2433024 | tf_op jit(solution)/shard_map/reduce_scatter | solution.py:262
  12.2 58.0 %copy-start = (bf16[12,784,64]{1,2,0:T(8,128)(2,1)}, bf16[12,784,64]{1,2,0:T(8,128)(2,1)S(1)}, u32[]{:S(2)}) copy-start(bf16[12,784,64]{1,2,0:T(8,128)(2,1)S(1)} %fusion.94) | copy-start | bytes 3612676
  302.3 114.8 %copy-start.17 = (bf16[1,784,768]{2,1,0:T(8,128)(2,1)S(1)}, bf16[1,784,768]{2,1,0:T(8,128)(2,1)}, u32[]{:S(2)}) copy-start(bf16[1,784,768]{2,1,0:T(8,128)(2,1)} %param.27) | copy-start | bytes 3612676
  417.0 9.8 copy-start.23
  426.8 2.7 copy-start.11
  426.8 3.3 copy-start.10
  426.9 3.5 copy-start.7
  426.9 4.9 copy-start.24
  434.9 2.1 copy-start.16
  437.1 2.9 copy-start.25
  439.9 228.7 %reduce-scatter.10.cloned.1.call-start = ((), (), s32[]{:S(2)}) async-start(), calls=%async_computation.15 | async-start | bytes 2433024 | tf_op jit(solution)/shard_map/reduce_scatter | solution.py:260
  443.8 2.8 copy-start.1
  570.5 201.9 %reduce-scatter.8.cloned.1.call-start = ((), (), s32[]{:S(2)}) async-start(), calls=%async_computation.14 | async-start | bytes 2433024 | tf_op jit(solution)/shard_map/reduce_scatter | solution.py:259
  570.5 2.5 copy-start.4
  576.2 301.0 %reduce-scatter.12.cloned.1.call-start = ((), (), s32[]{:S(2)}) async-start(), calls=%async_computation.16 | async-start | bytes 2433024 | tf_op jit(solution)/shard_map/reduce_scatter | solution.py:261
  580.7 415.9 %reduce-scatter.16.cloned.1.call-start = ((), (), s32[]{:S(2)}) async-start(), calls=%async_computation.18 | async-start | bytes 6488064 | tf_op jit(solution)/shard_map/reduce_scatter | solution.py:193
  588.0 529.5 %reduce-scatter.18.cloned.1.call-start = ((), (), s32[]{:S(2)}) async-start(), calls=%async_computation.19 | async-start | bytes 6488064 | tf_op jit(solution)/shard_map/reduce_scatter | solution.py:194
  595.4 642.0 %reduce-scatter.20.cloned.1.call-start = ((), (), s32[]{:S(2)}) async-start(), calls=%async_computation.20 | async-start | bytes 6488064 | tf_op jit(solution)/shard_map/reduce_scatter | solution.py:195
  606.1 2.8 copy-start.15
  606.1 2.8 copy-start.20
  608.9 1.6 copy-start.19
  653.6 4.3 copy-start.8
  653.6 4.3 copy-start.22
  (8 other events, 10.7 us)
Sparse Core Ops, SparseCore 0:
  10.9 56.7 all-gather.9
  70.6 52.9 all-gather.7
  126.5 52.9 all-gather.11
  182.3 52.9 all-gather.13
  238.0 57.8 all-gather.15
  298.6 57.7 all-gather.17
  359.2 57.7 all-gather.19
  440.0 97.8 reduce-scatter.13
  570.6 97.9 reduce-scatter.9
  674.3 98.0 reduce-scatter.7
  779.0 98.0 reduce-scatter.11
  883.2 113.3 reduce-scatter.15
  1003.7 113.7 reduce-scatter.17
  1123.5 113.8 reduce-scatter.19
where the time goes:
time: 1260 us; the launch traced here: 1240 us
  waiting for transfers between devices  842 us (67%)
  matrix products  248 us (20%)
  blocking collectives  80.7 us (6%)
  local copies, waits for them, and re-layouts  32.3 us (3%)
  other arithmetic  25.2 us (2%)
  between operations  14.7 us (1%)
    reduce_scatter x1, waiting for transfers between devices, per_device(): lax.psum_scatter(up_grad, 'fsdp', scatter_dimension=0, tiled=True)  121 us
    reduce_scatter x1, waiting for transfers between devices, per_device(): lax.psum_scatter(down_grad, 'fsdp', scatter_dimension=0, tiled=True)  120 us
    reduce_scatter x1, waiting for transfers between devices, per_device(): lax.psum_scatter(gate_grad, 'fsdp', scatter_dimension=0, tiled=True)  119 us
    reduce_scatter x1, waiting for transfers between devices, per_device(): lax.psum_scatter(value_grad, 'fsdp', scatter_dimension=0, tiled=True)  105 us
    reduce_scatter x1, waiting for transfers between devices, per_device(): lax.psum_scatter(query_grad, 'fsdp', scatter_dimension=0, tiled=True)  104 us
    unnamed x2, blocking collectives  80.7 us
    all_gather x1, waiting for transfers between devices, per_device(): lax.all_gather(w_down, 'fsdp', axis=0, tiled=True)  54.1 us
    all_gather x1, waiting for transfers between devices, per_device(): lax.all_gather(w_up, 'fsdp', axis=0, tiled=True)  54.1 us
  transfers between devices with their start and end apart: 14, of which 12 were waited for; matrix products, arithmetic and copies ran while one was open for 22% of the time, Pallas kernels for 0%

commit v1 on v0

v1 whole, which is shorter than its diff:
```python
from functools import partial

import jax
import jax.numpy as jnp
from jax import lax
from jax.experimental import pallas as pl
from jax.experimental.pallas import tpu as pltpu
from jax.sharding import PartitionSpec as P

HEAD = 64
EPSILON = 1e-05
CELLS = 32
MESH = pl.DeviceIdType.MESH
F32 = jnp.float32
BF16 = jnp.bfloat16


def place(fold):
    me = lax.axis_index("fsdp")
    cell = me // fold
    k = cell % 2
    x = (cell // 2) % 2
    y = (cell // 4) % 2
    z = cell // 8
    ids = {
        "core": me + (1 - 2 * k) * fold,
        "x": me + (1 - 2 * x) * (2 * fold),
        "y": me + (1 - 2 * y) * (4 * fold),
    }
    for r in (1, 2, 3):
        ids[r] = me + ((z + r) % 4 - z) * (8 * fold)
    return z, y, x, k, ids


def greet(ids):
    barrier = pltpu.get_barrier_semaphore()
    for peer in ids.values():
        pl.semaphore_signal(barrier, inc=1, device_id=(peer,), device_id_type=MESH)
    pl.semaphore_wait(barrier, len(ids))


class Gather:
    def __init__(self, where, own, full, send, recv, local):
        self.where, self.own, self.full = where, own, full
        self.send, self.recv, self.local = send, recv, local
        self.half = full.shape[-1] // 2
        self.copies = {}

    def push(self, slot, src, dst, peer):
        copy = pltpu.make_async_remote_copy(
            src_ref=src,
            dst_ref=dst,
            send_sem=self.send.at[slot],
            recv_sem=self.recv.at[slot],
            device_id=(peer,),
            device_id_type=MESH,
        )
        copy.start()
        self.copies[slot] = copy

    def arrive(self, *slots):
        for slot in slots:
            self.copies[slot].wait_recv()

    def step0(self):
        z, y, x, k, ids = self.where
        self.keep = pltpu.make_async_copy(self.own, self.full.at[z, y, x, k], self.local)
        self.keep.start()
        for r in (2, 1, 3):
            self.push(r - 1, self.own, self.full.at[z, y, x, k], ids[r])

    def step1(self):
        z, y, x, k, ids = self.where
        h, n = self.half, self.full.shape[-1]
        self.keep.wait()
        self.arrive(0, 1, 2)
        a = self.full.at[:, y, x, k, :, pl.ds(0, h)]
        b = self.full.at[:, y, x, k, :, pl.ds(h, n - h)]
        self.push(3, a, a, ids["y"])
        self.push(4, b, b, ids["x"])

    def step2(self):
        z, y, x, k, ids = self.where
        h, n = self.half, self.full.shape[-1]
        self.arrive(3, 4)
        a = self.full.at[:, :, x, k, :, pl.ds(0, h)]
        b = self.full.at[:, y, :, k, :, pl.ds(h, n - h)]
        self.push(5, a, a, ids["x"])
        self.push(6, b, b, ids["y"])

    def step3(self):
        z, y, x, k, ids = self.where
        self.arrive(5, 6)
        part = self.full.at[:, :, :, k]
        self.push(7, part, part, ids["core"])

    def step4(self):
        self.arrive(7)

    def settle(self):
        for copy in self.copies.values():
            copy.wait_send()


class Scatter:
    def __init__(self, where, full, bufs, send, recv):
        self.where, self.full = where, full
        self.r0, self.r1, self.r2, self.r3 = bufs
        self.send, self.recv = send, recv
        self.half = full.shape[-1] // 2
        self.copies = {}

    push = Gather.push
    arrive = Gather.arrive
    settle = Gather.settle

    def step0(self):
        z, y, x, k, ids = self.where
        self.push(0, self.full.at[:, :, :, 1 - k], self.r0, ids["core"])

    def step1(self):
        z, y, x, k, ids = self.where
        h, n = self.half, self.full.shape[-1]
        self.arrive(0)

        def add(i, _):
            a, b, c = i // 4, (i // 2) % 2, i % 2
            self.r0[a, b, c] = (
                self.r0[a, b, c].astype(F32) + self.full[a, b, c, k].astype(F32)
            ).astype(BF16)
            return 0

        lax.fori_loop(0, 16, add, 0)
        self.push(
            1, self.r0.at[:, :, 1 - x, :, pl.ds(0, h)], self.r1.at[:, :, :, pl.ds(0, h)], ids["x"]
        )
        self.push(
            2,
            self.r0.at[:, 1 - y, :, :, pl.ds(h, n - h)],
            self.r1.at[:, :, :, pl.ds(h, n - h)],
            ids["y"],
        )

    def step2(self):
        z, y, x, k, ids = self.where
        h, n = self.half, self.full.shape[-1]
        self.arrive(1, 2)

        def add(i, _):
            a, b = i // 2, i % 2
            self.r1[a, b, :, :h] = (
                self.r1[a, b, :, :h].astype(F32) + self.r0[a, b, x, :, :h].astype(F32)
            ).astype(BF16)
            self.r1[a, b, :, h:] = (
                self.r1[a, b, :, h:].astype(F32) + self.r0[a, y, b, :, h:].astype(F32)
            ).astype(BF16)
            return 0

        lax.fori_loop(0, 8, add, 0)
        self.push(
            3, self.r1.at[:, 1 - y, :, pl.ds(0, h)], self.r2.at[:, :, pl.ds(0, h)], ids["y"]
        )
        self.push(
            4,
            self.r1.at[:, 1 - x, :, pl.ds(h, n - h)],
            self.r2.at[:, :, pl.ds(h, n - h)],
            ids["x"],
        )

    def step3(self):
        z, y, x, k, ids = self.where
        h = self.half
        self.arrive(3, 4)

        def add(a, _):
            self.r2[a, :, :h] = (
                self.r2[a, :, :h].astype(F32) + self.r1[a, y, :, :h].astype(F32)
            ).astype(BF16)
            self.r2[a, :, h:] = (
                self.r2[a, :, h:].astype(F32) + self.r1[a, x, :, h:].astype(F32)
            ).astype(BF16)
            return 0

        lax.fori_loop(0, 4, add, 0)
        for r in (2, 1, 3):
            self.push(4 + r, self.r2.at[(z + r) % 4], self.r3.at[r - 1], ids[r])

    def step4(self):
        z = self.where[0]
        self.arrive(5, 6, 7)
        return (
            self.r2[z].astype(F32)
            + self.r3[0].astype(F32)
            + self.r3[1].astype(F32)
            + self.r3[2].astype(F32)
        )


def gather_kernel(fold, count, *refs):
    owns, fulls = refs[:count], refs[count : 2 * count]
    send, recv, local = refs[2 * count :]
    where = place(fold)
    greet(where[4])
    groups = [
        Gather(where, owns[i], fulls[i], send.at[i], recv.at[i], local.at[i]) for i in range(count)
    ]
    for t in range(count + 4):
        for i in range(count):
            if 0 <= t - i <= 4:
                getattr(groups[i], "step%d" % (t - i))()
    for group in groups:
        group.settle()


def scatter_kernel(fold, count, *refs):
    fulls_hbm, outs = refs[:count], refs[count : 2 * count]
    bufs = refs[2 * count : 7 * count]
    send, recv, local = refs[7 * count :]
    where = place(fold)
    greet(where[4])
    groups, loads = [], []
    for i in range(count):
        full, *rest = bufs[5 * i : 5 * i + 5]
        loads.append(pltpu.make_async_copy(fulls_hbm[i], full, local.at[i]))
        loads[-1].start()
        groups.append(Scatter(where, full, rest, send.at[i], recv.at[i]))
    for t in range(count + 4):
        for i in range(count):
            s = t - i
            if s == 0:
                loads[i].wait()
            if 0 <= s < 4:
                getattr(groups[i], "step%d" % s)()
            if s == 4:
                outs[i][...] = groups[i].step4()
    for group in groups:
        group.settle()


def gather_all(fold, blocks):
    count = len(blocks)
    shapes = [(4, 2, 2, 2) + b.shape for b in blocks]
    fulls = pl.pallas_call(
        partial(gather_kernel, fold, count),
        out_shape=[jax.ShapeDtypeStruct(s, BF16) for s in shapes],
        in_specs=[pl.BlockSpec(memory_space=pl.ANY)] * count,
        out_specs=[pl.BlockSpec(memory_space=pl.ANY)] * count,
        scratch_shapes=[
            pltpu.SemaphoreType.DMA((count, 8)),
            pltpu.SemaphoreType.DMA((count, 8)),
            pltpu.SemaphoreType.DMA((count,)),
        ],
        compiler_params=pltpu.CompilerParams(
            collective_id=0, has_side_effects=True, vmem_limit_bytes=8 * 2**20
        ),
    )(*blocks)
    return [f.reshape(-1, f.shape[-1]) for f in fulls]


def scatter_all(fold, parts):
    count = len(parts)
    fulls = [p.reshape(4, 2, 2, 2, p.shape[0] // CELLS, p.shape[1]) for p in parts]
    scratch = []
    for f in fulls:
        r, c = f.shape[-2:]
        for lead in ((4, 2, 2, 2), (4, 2, 2), (4, 2), (4,), (3,)):
            scratch.append(pltpu.VMEM(lead + (r, c), BF16))
    return pl.pallas_call(
        partial(scatter_kernel, fold, count),
        out_shape=[jax.ShapeDtypeStruct(f.shape[-2:], F32) for f in fulls],
        in_specs=[pl.BlockSpec(memory_space=pl.ANY)] * count,
        out_specs=[pl.BlockSpec(memory_space=pltpu.VMEM)] * count,
        scratch_shapes=scratch
        + [
            pltpu.SemaphoreType.DMA((count, 8)),
            pltpu.SemaphoreType.DMA((count, 8)),
            pltpu.SemaphoreType.DMA((count,)),
        ],
        compiler_params=pltpu.CompilerParams(
            collective_id=1, has_side_effects=True, vmem_limit_bytes=58 * 2**20
        ),
    )(*fulls)


def rope_tables(segment_row, head_size):
    length = segment_row.shape[0]
    places = jnp.arange(length, dtype=jnp.int32)
    labels = jnp.arange(4, dtype=jnp.int32)
    counts = jnp.sum((segment_row[:, None] == labels[None, :]).astype(jnp.int32), axis=0)
    before = (labels[None, :] < segment_row[:, None]).astype(jnp.int32)
    starts = jnp.sum(before * counts[None, :], axis=1)
    offsets = (places - starts).astype(F32)
    frequency = 10000.0 ** (-(jnp.arange(head_size // 2, dtype=F32) * 2.0) / head_size)
    angles = offsets[:, None] * frequency[None, :]
    return (jnp.cos(angles), jnp.sin(angles))


def rotate(values, cosine, sine_table):
    half_size = values.shape[-1] // 2
    lower_half = values[..., :half_size]
    upper_half = values[..., half_size:]
    cosine = cosine[..., None, :]
    sine_table = sine_table[..., None, :]
    return jnp.concatenate(
        [
            lower_half * cosine - upper_half * sine_table,
            upper_half * cosine + lower_half * sine_table,
        ],
        axis=-1,
    )


def unrotate(gradient, cosine, sine_table):
    half_size = gradient.shape[-1] // 2
    lower_half = gradient[..., :half_size]
    upper_half = gradient[..., half_size:]
    cosine = cosine[..., None, :]
    sine_table = sine_table[..., None, :]
    return jnp.concatenate(
        [
            lower_half * cosine + upper_half * sine_table,
            upper_half * cosine - lower_half * sine_table,
        ],
        axis=-1,
    )


def head_forward(query_head, key_head, value_head, allowed, score_scale):
    raw_scores = jnp.einsum("le,me->lm", query_head, key_head, preferred_element_type=F32)
    masked = jnp.where(allowed, raw_scores * score_scale, -1e30)
    highest = jnp.max(masked, axis=-1, keepdims=True)
    exponent = jnp.exp(masked - highest)
    denominator = jnp.sum(exponent, axis=-1, keepdims=True)
    weights = (exponent / denominator).astype(BF16)
    mixture = jnp.dot(weights, value_head, preferred_element_type=F32)
    return (mixture, (highest + jnp.log(denominator))[:, 0])


def head_backward(query_head, key_head, value_head, grad_head, logsum, allowed, score_scale):
    raw_scores = jnp.einsum("le,me->lm", query_head, key_head, preferred_element_type=F32)
    masked = jnp.where(allowed, raw_scores * score_scale, -1e30)
    probabilities = jnp.exp(masked - logsum[:, None])
    weights = probabilities.astype(BF16)
    grad_value = jnp.einsum("lm,le->me", weights, grad_head, preferred_element_type=F32)
    grad_probs = jnp.einsum("le,me->lm", grad_head, value_head, preferred_element_type=F32)
    grad_scores = probabilities * (
        grad_probs - jnp.sum(grad_probs * probabilities, axis=-1, keepdims=True)
    )
    grad_scores = grad_scores.astype(BF16)
    grad_query = jnp.dot(grad_scores, key_head, preferred_element_type=F32) * score_scale
    grad_key = (
        jnp.einsum("lm,le->me", grad_scores, query_head, preferred_element_type=F32)
        * score_scale
    )
    return (grad_query, grad_key, grad_value)


def fold_groups(fold):
    return [[c * fold + j for j in range(fold)] for c in range(CELLS)]


def norm_backward(scaled, normed, inverse):
    return inverse * (scaled - normed * jnp.mean(scaled * normed, axis=-1, keepdims=True))


def per_device(
    fold,
    block_input,
    seg_ids,
    gain_attn,
    w_query,
    w_key,
    w_value,
    w_out,
    gain_ffn,
    w_gate,
    w_up,
    w_down,
    cotangent,
):
    row_count, length, width = block_input.shape
    head_count = width // HEAD
    tokens = row_count * length
    score_scale = HEAD ** (-0.5)
    groups = fold_groups(fold)
    gain_one = gain_attn.astype(F32)[:, None]
    gain_two = gain_ffn.astype(F32)[:, None]
    blocks = [
        (w.astype(F32) * gain_one).astype(BF16) for w in (w_query, w_key, w_value)
    ] + [w_out, w_down] + [(w.astype(F32) * gain_two).astype(BF16) for w in (w_gate, w_up)]
    if fold > 1:
        blocks = [
            lax.all_gather(w, "fsdp", axis=0, tiled=True, axis_index_groups=groups) for w in blocks
        ]
    wq, wk, wv, wo, wd, wg, wu = gather_all(fold, blocks)
    cosine, sine_table = jax.vmap(partial(rope_tables, head_size=HEAD))(seg_ids)
    places = jnp.arange(length, dtype=jnp.int32)
    allowed = (seg_ids[:, :, None] == seg_ids[:, None, :]) & (
        places[None, None, :] <= places[None, :, None]
    )
    inputs = block_input.reshape(tokens, width).astype(F32)
    scale_one = lax.rsqrt(jnp.mean(inputs * inputs, axis=-1, keepdims=True) + EPSILON)
    normed_one = inputs * scale_one
    normed_low = normed_one.astype(BF16)
    queries = jnp.dot(normed_low, wq, preferred_element_type=F32).reshape(
        row_count, length, head_count, HEAD
    )
    key_vectors = jnp.dot(normed_low, wk, preferred_element_type=F32).reshape(
        row_count, length, head_count, HEAD
    )
    value_vectors = jnp.dot(normed_low, wv, preferred_element_type=F32).astype(
        BF16
    )
    value_vectors = value_vectors.reshape(row_count, length, head_count, HEAD)
    query_rot = rotate(queries, cosine, sine_table).astype(BF16)
    key_rot = rotate(key_vectors, cosine, sine_table).astype(BF16)
    query_heads = jnp.moveaxis(query_rot, 2, 1)
    key_heads = jnp.moveaxis(key_rot, 2, 1)
    value_heads = jnp.moveaxis(value_vectors, 2, 1)

    def row_forward(operands):
        query_row, key_row, value_row, allowed_row = operands

        def one_head(head_parts):
            return head_forward(
                head_parts[0], head_parts[1], head_parts[2], allowed_row, score_scale
            )

        return lax.map(one_head, (query_row, key_row, value_row))

    mixture, logsum = lax.map(row_forward, (query_heads, key_heads, value_heads, allowed))
    attn_low = jnp.moveaxis(mixture, 1, 2).reshape(tokens, width).astype(BF16)
    middle = inputs + jnp.dot(attn_low, wo, preferred_element_type=F32)
    scale_two = lax.rsqrt(jnp.mean(middle * middle, axis=-1, keepdims=True) + EPSILON)
    normed_two = middle * scale_two
    ffn_low = normed_two.astype(BF16)
    gate_proj = jnp.dot(ffn_low, wg, preferred_element_type=F32)
    up_proj = jnp.dot(ffn_low, wu, preferred_element_type=F32)
    gate_sigm = jax.nn.sigmoid(gate_proj)
    activated = gate_proj * gate_sigm
    hidden = (activated * up_proj).astype(BF16)
    output_full = middle + jnp.dot(hidden, wd, preferred_element_type=F32)
    output = output_full.astype(BF16).reshape(row_count, length, width)
    grad_out = cotangent.reshape(tokens, width).astype(F32)
    grad_low = grad_out.astype(BF16)
    down_grad = jnp.einsum("tf,td->fd", hidden, grad_low, preferred_element_type=F32)
    grad_hidden = jnp.einsum("td,fd->tf", grad_low, wd, preferred_element_type=F32)
    gate_grad_low = (
        grad_hidden * up_proj * gate_sigm * (1.0 + gate_proj * (1.0 - gate_sigm))
    ).astype(BF16)
    up_grad_low = (grad_hidden * activated).astype(BF16)
    gate_grad = jnp.einsum("td,tf->df", ffn_low, gate_grad_low, preferred_element_type=F32)
    up_grad = jnp.einsum("td,tf->df", ffn_low, up_grad_low, preferred_element_type=F32)
    grad_normed_two = jnp.einsum(
        "tf,df->td", gate_grad_low, wg, preferred_element_type=F32
    )
    grad_normed_two = grad_normed_two + jnp.einsum(
        "tf,df->td", up_grad_low, wu, preferred_element_type=F32
    )
    grad_middle = grad_out + norm_backward(
        grad_normed_two, normed_two, scale_two
    )
    branch_low = grad_middle.astype(BF16)
    out_grad = jnp.einsum("te,td->ed", attn_low, branch_low, preferred_element_type=F32)
    grad_attn = jnp.einsum(
        "td,ed->te", branch_low, wo, preferred_element_type=F32
    ).astype(BF16)
    grad_heads = jnp.moveaxis(grad_attn.reshape(row_count, length, head_count, HEAD), 2, 1)

    def row_backward(operands):
        query_row, key_row, value_row, grad_row, logsum_row, allowed_row = operands

        def one_head(head_parts):
            return head_backward(
                head_parts[0],
                head_parts[1],
                head_parts[2],
                head_parts[3],
                head_parts[4],
                allowed_row,
                score_scale,
            )

        return lax.map(one_head, (query_row, key_row, value_row, grad_row, logsum_row))

    grad_query_heads, grad_key_heads, grad_value_heads = lax.map(
        row_backward, (query_heads, key_heads, value_heads, grad_heads, logsum, allowed)
    )
    query_grad_low = (
        unrotate(jnp.moveaxis(grad_query_heads, 1, 2), cosine, sine_table)
        .reshape(tokens, width)
        .astype(BF16)
    )
    key_grad_low = (
        unrotate(jnp.moveaxis(grad_key_heads, 1, 2), cosine, sine_table)
        .reshape(tokens, width)
        .astype(BF16)
    )
    value_grad_low = (
        jnp.moveaxis(grad_value_heads, 1, 2).reshape(tokens, width).astype(BF16)
    )
    query_grad = jnp.einsum(
        "td,te->de", normed_low, query_grad_low, preferred_element_type=F32
    )
    key_grad = jnp.einsum("td,te->de", normed_low, key_grad_low, preferred_element_type=F32)
    value_grad = jnp.einsum(
        "td,te->de", normed_low, value_grad_low, preferred_element_type=F32
    )
    grad_normed_one = jnp.einsum(
        "te,de->td", query_grad_low, wq, preferred_element_type=F32
    )
    grad_normed_one = grad_normed_one + jnp.einsum(
        "te,de->td", key_grad_low, wk, preferred_element_type=F32
    )
    grad_normed_one = grad_normed_one + jnp.einsum(
        "te,de->td", value_grad_low, wv, preferred_element_type=F32
    )
    input_full = grad_middle + norm_backward(
        grad_normed_one, normed_one, scale_one
    )
    input_grad = input_full.astype(BF16).reshape(row_count, length, width)
    parts = scatter_all(
        fold,
        [
            g.astype(BF16)
            for g in (query_grad, key_grad, value_grad, out_grad, down_grad, gate_grad, up_grad)
        ],
    )
    if fold > 1:
        parts = [
            lax.psum_scatter(
                g, "fsdp", scatter_dimension=0, tiled=True, axis_index_groups=groups
            )
            for g in parts
        ]
    dq, dk, dv, do, dd, dg, du = parts
    gain_one_grad = sum(
        jnp.sum(w.astype(F32) * g, axis=1)
        for w, g in ((w_query, dq), (w_key, dk), (w_value, dv))
    )
    gain_two_grad = sum(
        jnp.sum(w.astype(F32) * g, axis=1) for w, g in ((w_gate, dg), (w_up, du))
    )
    return (
        output,
        input_grad,
        gain_one_grad,
        dq * gain_one,
        dk * gain_one,
        dv * gain_one,
        do,
        gain_two_grad,
        dg * gain_two,
        du * gain_two,
        dd,
    )


def solution(mesh):
    fold = mesh.shape["fsdp"] // CELLS
    placed = (
        P("fsdp", None, None),
        P("fsdp", None),
        P("fsdp"),
        P("fsdp", None),
        P("fsdp", None),
        P("fsdp", None),
        P("fsdp", None),
        P("fsdp"),
        P("fsdp", None),
        P("fsdp", None),
        P("fsdp", None),
        P("fsdp", None, None),
    )
    return jax.shard_map(
        partial(per_device, fold),
        mesh=mesh,
        in_specs=placed,
        out_specs=(
            P("fsdp", None, None),
            P("fsdp", None, None),
            P("fsdp"),
            P("fsdp", None),
            P("fsdp", None),
            P("fsdp", None),
            P("fsdp", None),
            P("fsdp"),
            P("fsdp", None),
            P("fsdp", None),
            P("fsdp", None),
        ),
        check_vma=False,
    )
```

time: 1260 us -> 518 us (0.41)
  waiting for transfers between devices: 842 us -> 0 us
  Pallas kernels: 0 us -> 163 us
  blocking collectives: 80.7 us -> 0 us
  local copies, waits for them, and re-layouts: 32.3 us -> 55.8 us
  between operations: 14.7 us -> 1.61 us
    reduce_scatter x7 -> x0, waiting for transfers between devices: 574 us -> none  [the longest x1 121 us: per_device(): lax.psum_scatter(up_grad, 'fsdp', scatter_dimension=0, tiled=True)]
    all_gather x7 -> x0, waiting for transfers between devices: 264 us -> none  [the longest x1 54.1 us: per_device(): lax.all_gather(w_down, 'fsdp', axis=0, tiled=True)]
    pallas_call x0 -> x2, Pallas kernels: none -> 163 us  [the longest x1 82.5 us: scatter_all(): pl.pallas_call(partial(scatter_kernel, fold, count), out_shape=[jax.Shape...]
    unnamed x2 -> x0, blocking collectives: 80.7 us -> none
    while x0 -> x24, local copies, waits for them, and re-layouts: none -> 18.3 us
    unnamed x62 -> x98, local copies, waits for them, and re-layouts: 23.1 us -> 28.4 us
  transfers between devices with their start and end apart: 14 -> 0, of which waited for: 12 -> 0; matrix products, arithmetic and copies ran while one was open for 22% -> 0% of each run, Pallas kernels for 0% -> 0%
where the time goes in v1:
time: 518 us; the launch traced here: 508 us
  matrix products  253 us (49%)
  Pallas kernels  163 us (31%)
  local copies, waits for them, and re-layouts  55.8 us (11%)
  other arithmetic  33.5 us (6%)
    pallas_call x1, Pallas kernels, scatter_all(): pl.pallas_call(partial(scatter_kernel, fold, count), out_shape=[jax.Shape...  82.5 us
    pallas_call x1, Pallas kernels, gather_all(): pl.pallas_call(partial(gather_kernel, fold, count), out_shape=[jax.ShapeD...  80.9 us
    dot_general x12, matrix products, head_forward(): mixture = jnp.dot(weights, value_head, preferred_element_type=F32)  37 us
    unnamed x98, local copies, waits for them, and re-layouts  28.4 us
    dot_general x12, matrix products, head_backward(): jnp.einsum('lm,le->me', grad_scores, query_head, preferred_element_type=F32)  26.3 us
    dot_general x12, matrix products, head_backward(): jnp.einsum('lm,le->me', weights, grad_head, preferred_element_type=F32)  25.4 us
    dot_general x12, matrix products, head_backward(): jnp.dot(grad_scores, key_head, preferred_element_type=F32) * score_scale  24.5 us
    dot_general x12, matrix products, head_forward(): jnp.einsum('le,me->lm', query_head, key_head, preferred_element_type=F32)  21.2 us

profile of v1, /device:TPU:0, one launch (start us, length us, event | category | flops | bytes accessed | tf_op | source)
XLA Modules:
  0.0 508.1 jit_solution(13055754391292505256)
XLA Ops:
  5.6 80.9 %shard_map.206 = (bf16[4,2,2,2,24,768]{5,4,3,2,1,0:T(8,128)(2,1)S(1)}, bf16[4,2,2,2,24,768]{5,4,3,2,1,0:T(8,128)(2,1)S(1)}, bf16[4,2,2,2,24,768]{5,4,3,2,1,0:T(8...) custom-call(bf16[24,768]{1,0:T(8,128)(2,1)S(1)} %get-tuple-element.3, ...), custom_call_target="tpu_custom_call" | custom-call | tf_op jit(solution)/shard_map/pallas_call | solution.py:243
  96.1 4.7 convolution_bitcast_fusion
  101.5 4.3 convolution_bitcast_fusion.1
  106.6 3.4 subtract_convert_fusion.2
  114.0 4.0 copy.46
  122.7 3.9 copy.47
  130.4 83.6 %while.50 = (s32[]{:T(128)}, bf16[12,784,64]{1,2,0:T(8,128)(2,1)}, f32[12,784]{1,0:T(8,128)S(1)}, bf16[12,784,64]{2,1,0:T(8,128)(2,1)}, bf16[12,784,64]{2,1,0:T(...) while((s32[]{:T(128)}, bf16[12,784,64]{1,2,0:T(8,128)(2,1)}, ...), condition=%wide.region_6.7_spmd.clone.clone, body=%wide.region_3.6_spmd.clone.sunk.clone | while | flops 164112368 | bytes 18441068 | solution.py:429
  134.4 3.1 fusion.170
  141.3 3.1 fusion.170
  148.3 3.1 fusion.170
  155.2 3.1 fusion.170
  162.1 3.1 fusion.170
  169.1 3.1 fusion.170
  176.0 3.1 fusion.170
  183.0 3.1 fusion.170
  189.9 3.1 fusion.170
  196.9 3.1 fusion.170
  203.8 3.1 fusion.170
  210.8 3.1 fusion.170
  222.1 4.5 fusion.98
  226.6 9.4 %fusion.53 = (bf16[784,2048]{1,0:T(8,128)(2,1)}, bf16[784,2048]{1,0:T(8,128)(2,1)}, bf16[784,2048]{1,0:T(8,128)(2,1)}) fusion(f32[784,2048]{1,0:T(8,128)} %fusion.98, f32[784,2048]{1,0:T(8,128)S(1)} %fusion.99, bf16[2048,768]{1,0:T(8,128)(2,1)S(1)} %bitcast.264, bf16[1,784,768]{2,1,0:T(8,128)(2,1)S(1)} %copy-done.29), kind=kOutput, calls=%fused_computation.61 | convolution fusion | flops 2490335232 | bytes 26828800 | tf_op jit(solution)/shard_map/td,fd->tf/dot_general | solution.py:447
  236.1 6.9 %convolution_convert_fusion = bf16[768,2048]{1,0:T(8,128)(2,1)} fusion(bf16[784,768]{1,0:T(8,128)(2,1)S(1)} %multiply_convert_fusion.2, bf16[784,2048]{1,0:T(8,128)(2,1)} %get-tuple-element.316), kind=kOutput, calls=%fused_computation.65 | convolution fusion | flops 2467823616 | bytes 7561216 | tf_op jit(solution)/shard_map/td,tf->df/dot_general | solution.py:453
  242.9 5.1 %convolution_convert_fusion.1 = bf16[768,2048]{1,0:T(8,128)(2,1)} fusion(bf16[784,768]{1,0:T(8,128)(2,1)S(1)} %multiply_convert_fusion.2, bf16[784,2048]{1,0:T(8,128)(2,1)S(1)} %copy-done.46), kind=kOutput, calls=%fused_computation.66 | convolution fusion | flops 2467823616 | bytes 7561216 | tf_op jit(solution)/shard_map/td,tf->df/dot_general | solution.py:452
  250.8 3.0 multiply_reduce_fusion.1
  262.2 122.2 %while.51 = (s32[]{:T(128)}, f32[12,784,64]{1,2,0:T(8,128)}, f32[12,784,64]{1,2,0:T(8,128)}, bf16[12,784,64]{1,2,0:T(8,128)(2,1)}, bf16[12,784,64]{2,1,0:T(8,128...) while((s32[]{:T(128)}, f32[12,784,64]{1,2,0:T(8,128)}, ...), condition=%wide.region_11.12_spmd.clone.clone, body=%wide.region_9.11_spmd.clone.sunk.clone | while | flops 400855296 | bytes 20390760 | solution.py:484
  384.5 3.4 add_convert_fusion.1
  395.0 4.2 convolution_convert_fusion.6
  399.2 5.0 convolution_convert_fusion.2
  404.3 82.5 %shard_map.207 = (f32[24,768]{1,0:T(8,128)}, f32[24,768]{1,0:T(8,128)}, f32[24,768]{1,0:T(8,128)}, f32[24,768]{1,0:T(8,128)}, f32[64,768]{1,0:T(8,128)}, /*index=5*/f32[24,2048]{1,0:T(8,128)}, f32[24,2048]{1,0:T(8,128)}) custom-call(bf16[4,2,2,2,24,768]{5,4,3,2,1,0:T(8,128)(2,1)} %bitcast.287, bf16[4,2,2,2,24,768]{5,4,3,2,1,0:T(8,128)(2,1)} %bitcast.286, ...), custom_call_target="tpu_custom_call" | custom-call | tf_op jit(solution)/shard_map/pallas_call | solution.py:268
  491.7 2.8 fusion.102
  496.2 3.3 fusion.60
  502.6 3.7 fusion.67
  (306 shorter events, 233.5 us)
Async XLA Ops:
  92.6 8.2 %copy-start.2 = (bf16[4,2,2,2,24,768]{5,4,3,2,1,0:T(8,128)(2,1)}, bf16[4,2,2,2,24,768]{5,4,3,2,1,0:T(8,128)(2,1)S(1)}, u32[]{:S(2)}) copy-start(bf16[4,2,2,2,24,768]{5,4,3,2,1,0:T(8,128)(2,1)S(1)} %get-tuple-element.169) | copy-start | bytes 3538948
  92.6 8.2 %copy-start = (bf16[4,2,2,2,24,768]{5,4,3,2,1,0:T(8,128)(2,1)}, bf16[4,2,2,2,24,768]{5,4,3,2,1,0:T(8,128)(2,1)S(1)}, u32[]{:S(2)}) copy-start(bf16[4,2,2,2,24,768]{5,4,3,2,1,0:T(8,128)(2,1)S(1)} %get-tuple-element.168) | copy-start | bytes 3538948
  92.6 25.4 %copy-start.4 = (bf16[4,2,2,2,24,768]{5,4,3,2,1,0:T(8,128)(2,1)}, bf16[4,2,2,2,24,768]{5,4,3,2,1,0:T(8,128)(2,1)S(1)}, u32[]{:S(2)}) copy-start(bf16[4,2,2,2,24,768]{5,4,3,2,1,0:T(8,128)(2,1)S(1)} %get-tuple-element.170) | copy-start | bytes 3538948
  101.5 4.4 copy-start.38
  114.0 4.0 copy-start.18
  130.4 83.6 %copy-start.15 = (bf16[4,2,2,2,24,768]{5,4,3,2,1,0:T(8,128)(2,1)S(1)}, bf16[4,2,2,2,24,768]{5,4,3,2,1,0:T(8,128)(2,1)}, u32[]{:S(2)}) copy-start(bf16[4,2,2,2,24,768]{5,4,3,2,1,0:T(8,128)(2,1)} %copy-done.14) | copy-start | bytes 3538948
  216.7 37.1 %copy-start.21 = (f32[784,768]{1,0:T(8,128)}, f32[784,768]{1,0:T(8,128)S(1)}, u32[]{:S(2)}) copy-start(f32[784,768]{1,0:T(8,128)S(1)} %get-tuple-element.357) | copy-start | bytes 7225348
  216.7 2.8 copy-start.11
  219.4 2.7 copy-start.13
  222.1 4.5 copy-start.9
  222.1 4.5 copy-start.29
  236.0 6.9 %copy-start.46 = (bf16[784,2048]{1,0:T(8,128)(2,1)S(1)}, bf16[784,2048]{1,0:T(8,128)(2,1)}, u32[]{:S(2)}) copy-start(bf16[784,2048]{1,0:T(8,128)(2,1)} %get-tuple-element.317) | copy-start | bytes 9633796
  248.0 2.7 copy-start.43
  255.1 2.5 copy-start.16
  388.1 4.0 copy-start.25
  392.3 2.7 copy-start.26
  395.0 4.2 copy-start.30
  395.0 4.2 copy-start.44
  404.2 82.6 %copy-start.31 = (bf16[24,2048]{1,0:T(8,128)(2,1)S(1)}, bf16[24,2048]{1,0:T(8,128)(2,1)}, u32[]{:S(2)}) copy-start(bf16[24,2048]{1,0:T(8,128)(2,1)} %param.25) | copy-start | bytes 294916
  404.2 82.6 %copy-start.32 = (bf16[24,2048]{1,0:T(8,128)(2,1)S(1)}, bf16[24,2048]{1,0:T(8,128)(2,1)}, u32[]{:S(2)}) copy-start(bf16[24,2048]{1,0:T(8,128)(2,1)} %param.24) | copy-start | bytes 294916
  404.2 82.6 %copy-start.40 = (f32[24]{0:T(128)S(1)}, f32[24]{0:T(128)}, u32[]{:S(2)}) copy-start(f32[24]{0:T(128)} %copy-done.39) | copy-start | bytes 292
  404.2 85.1 %copy-start.34 = (bf16[24,768]{1,0:T(8,128)(2,1)S(1)}, bf16[24,768]{1,0:T(8,128)(2,1)}, u32[]{:S(2)}) copy-start(bf16[24,768]{1,0:T(8,128)(2,1)} %param.21) | copy-start | bytes 110596
  404.2 85.1 %copy-start.35 = (bf16[24,768]{1,0:T(8,128)(2,1)S(1)}, bf16[24,768]{1,0:T(8,128)(2,1)}, u32[]{:S(2)}) copy-start(bf16[24,768]{1,0:T(8,128)(2,1)} %param.20) | copy-start | bytes 110596
  404.2 85.1 %copy-start.36 = (bf16[24,768]{1,0:T(8,128)(2,1)S(1)}, bf16[24,768]{1,0:T(8,128)(2,1)}, u32[]{:S(2)}) copy-start(bf16[24,768]{1,0:T(8,128)(2,1)} %param.19) | copy-start | bytes 110596
  404.3 85.0 %copy-start.42 = (f32[24]{0:T(128)S(1)}, f32[24]{0:T(128)}, u32[]{:S(2)}) copy-start(f32[24]{0:T(128)} %copy-done.41) | copy-start | bytes 292
  404.3 87.4 %copy-start.3 = (bf16[4,2,2,2,24,768]{5,4,3,2,1,0:T(8,128)(2,1)S(1)}, bf16[4,2,2,2,24,768]{5,4,3,2,1,0:T(8,128)(2,1)}, u32[]{:S(2)}) copy-start(bf16[4,2,2,2,24,768]{5,4,3,2,1,0:T(8,128)(2,1)} %copy-done.2) | copy-start | bytes 3538948
  491.7 2.8 copy-start.1
  491.7 2.9 copy-start.27
  496.2 3.3 copy-start.24
  499.5 3.1 copy-start.45
  502.6 3.7 copy-start.37
  502.6 4.3 copy-start.33
  (26 other events, 38.4 us)
